TPU v7x, 32 devices: a whole 2x2x4 slice. The times are simulated.
32 devices in a mesh: wide: 16 (over z, x, core), narrow: 2 (over y).
Axes of the slice: x: 2, y: 2, z: 4, core: 2. Of those that a mesh axis runs over, the one named last changes fastest.
Arguments:
- amplitudes: float32 [48, 1024, 1024], P('wide', None, 'narrow'), may hold values from -24 to 24
- integrals: float32 [16, 16, 1024, 1024], P('narrow', None, 'wide'), may hold values from -0.005859375 to 0.005859375
- pair_index: int32 [48, 2], P('wide'), may hold values from 0 to 199
- window_virtuals: int32 [16], replicated, may hold values from 0 to 1023
- occ_energy: float32 [200], replicated, may hold values from -3 to -0.5
- virt_energy: float32 [1024], replicated, may hold values from 0.3 to 6
Outputs:
- update: float32 [16, 16, 48], P('narrow', None, 'wide')
All inputs are finite; a program needn't handle non-finite values.
Results may differ from a plain program's by a relative error of at most 0.00013.
Values sent between devices are 32-bit elements; how exact they have to be, the bound alone decides.
No kernel may reach another device: no remote copies, remote signals or barrier semaphores. Data moves between devices by JAX's collectives and lax.ppermute only.
A program may use at most 128 MiB of HBM per device.

v0:
```python
import jax
import jax.numpy as jnp
from jax import lax
from jax.sharding import PartitionSpec as P


def lookup(table, indices):
    matches = (indices[..., None] == jnp.arange(table.shape[0], dtype=jnp.int32)).astype(
        jnp.float32
    )
    return jnp.sum(matches * table, axis=-1)


def contract(left_rows, right_rows):
    return lax.dot_general(
        left_rows.reshape(left_rows.shape[0], -1),
        right_rows.reshape(right_rows.shape[0], -1),
        (((1,), (1,)), ((), ())),
        precision=lax.Precision.HIGHEST,
        preferred_element_type=jnp.float32,
    )


def shards(amplitudes, integrals, pair_index, window_virtuals, occ_energy, virt_energy):
    exchanged = lax.all_to_all(amplitudes, "wide", split_axis=1, concat_axis=0, tiled=True)
    rows_here = integrals.shape[0]
    window = integrals.shape[1]
    first_block = integrals.shape[2]
    all_pairs = exchanged.shape[0]
    integral_rows = integrals.reshape(rows_here * window, first_block, integrals.shape[3])
    partial_value = contract(integral_rows, lax.all_gather(exchanged, "narrow", axis=2, tiled=True))
    ladder = lax.psum_scatter(
        partial_value.reshape(rows_here, window, all_pairs), "wide", scatter_dimension=2, tiled=True
    )
    swapped = lax.all_to_all(ladder, "narrow", split_axis=1, concat_axis=0, tiled=True)
    combined = ladder + jnp.transpose(swapped, (1, 0, 2))
    row_start = lax.axis_index("narrow") * rows_here
    own_virtuals = lax.dynamic_slice_in_dim(window_virtuals, row_start, rows_here, 0)
    row_energy = lookup(virt_energy, own_virtuals)
    column_energy = lookup(virt_energy, window_virtuals)
    pair_energy = lookup(occ_energy, pair_index[:, 0]) + lookup(occ_energy, pair_index[:, 1])
    denominator = (
        pair_energy[None, None, :] - row_energy[:, None, None] - column_energy[None, :, None]
    )
    return combined / denominator


def solution(mesh):
    in_specs = (
        P("wide", None, "narrow"),
        P("narrow", None, "wide", None),
        P("wide", None),
        P(),
        P(),
        P(),
    )
    out_specs = P("narrow", None, "wide")
    return jax.shard_map(shards, mesh=mesh, in_specs=in_specs, out_specs=out_specs, check_vma=False)
```

profile of v0, /device:TPU:0, one launch (start us, length us, event | category | flops | bytes accessed | tf_op | source)
XLA Modules:
  0.0 489.2 jit_solution(3291001078130395045)
XLA Ops:
  6.5 7.1 %copy.42 = f32[3,1024,512]{2,0,1:T(4,128)S(1)} copy(f32[3,1024,512]{2,1,0:T(8,128)} %param.6) | data formatting | bytes 12582912 | tf_op args[0]
  13.6 189.3 %all_to_all.36 = f32[3,1024,512]{2,0,1:T(4,128)S(1)} all-to-all(f32[3,1024,512]{2,0,1:T(4,128)S(1)} %copy.42), channel_id=1, replica_groups=mesh['wide'=16,'narrow'=2] {'wide'}, dimensions={1} | all-to-all | bytes 12582912 | tf_op jit(solution)/shard_map/all_to_all | solution.py:25
  202.9 2.0 copy.43
  205.0 1.2 copy.44
  206.2 0.0 copy-start.3
  206.2 0.0 copy-start.2
  206.2 0.0 copy-start.1
  206.2 0.0 copy-start
  206.3 6.3 %copy.45 = f32[48,64,512]{2,0,1:T(8,128)} copy(f32[48,64,512]{2,1,0:T(8,128)S(1)} %bitcast.30) | data formatting | bytes 12582912 | tf_op jit(solution)/shard_map/all_to_all | solution.py:25
  212.5 0.0 all-gather.2.cloned.1.call-update
  212.5 0.0 reduce-scatter.4.cloned.1.call-start
  212.6 0.1 dynamic_slice.3
  212.7 0.0 copy-done.2
  212.7 0.0 copy-done.1
  212.7 0.2 select_reduce_fusion.2
  212.9 0.2 select_reduce_fusion.1
  213.1 153.1 %all-gather.2.cloned.1.call-done = f32[48,64,1024]{2,0,1:T(8,128)} async-done(((f32[48,64,512]{2,0,1:T(8,128)}), f32[48,64,1024]{2,0,1:T(8,128)}) %all-gather.2.cloned.1.call-update) | async-done | bytes 12582928 | tf_op jit(solution)/shard_map/all_gather | solution.py:31
  366.2 50.3 %fusion.3 = f32[8,16,48]{2,1,0:T(8,128)S(1)} fusion(f32[48,64,1024]{2,0,1:T(8,128)} %all-gather.2.cloned.1.call-done, f32[8,16,64,1024]{3,2,1,0:T(8,128)} %param.7), kind=kOutput, calls=%fused_computation.3 | convolution fusion | flops 4831838208 | bytes 46161920 | tf_op jit(solution)/shard_map/dot_general | solution.py:15
  416.6 0.8 copy.47
  417.4 0.0 reduce-scatter.4.cloned.1.call-update
  417.4 0.1 broadcast_subtract_fusion
  417.5 53.7 %reduce-scatter.4.cloned.1.call-done = f32[8,16,3]{1,0,2:T(8,128)} async-done(((f32[8,16,48]{1,0,2:T(8,128)}), f32[8,16,3]{1,0,2:T(8,128)}) %reduce-scatter.4.cloned.1.call-update) | async-done | bytes 1552
  471.2 0.8 copy.48
  471.9 0.7 reshape.46
  472.6 3.2 all-to-all-start.1
  475.8 0.2 select_reduce_fusion
  476.0 3.6 all-to-all-done.1
  479.6 0.5 broadcast.40
  480.1 0.7 reduce
  480.8 0.1 reshape.47
  480.9 0.1 all_to_all.33
  481.0 1.4 fusion.8
  (6 shorter events, 0.0 us)
Async XLA Ops:
  6.5 359.7 %all-gather.2.cloned.1.call-start = ((), (), s32[]{:S(2)}) async-start(), calls=%async_computation.3 | async-start | bytes 18874368 | tf_op jit(solution)/shard_map/all_gather | solution.py:31
  206.2 6.4 %copy-start.3 = (s32[16]{0:T(128)S(1)}, s32[16]{0:T(128)}, u32[]{:S(2)}) copy-start(s32[16]{0:T(128)} %param.9) | copy-start | bytes 196
  206.2 6.5 %copy-start.2 = (s32[3,2]{0,1:T(2,128)S(1)}, s32[3,2]{0,1:T(2,128)}, u32[]{:S(2)}) copy-start(s32[3,2]{0,1:T(2,128)} %param.8) | copy-start | bytes 76
  206.2 6.5 %copy-start.1 = (f32[200]{0:T(256)S(1)}, f32[200]{0:T(256)}, u32[]{:S(2)}) copy-start(f32[200]{0:T(256)} %param.10) | copy-start | bytes 2404
  206.2 6.7 %copy-start = (f32[1024]{0:T(1024)S(1)}, f32[1024]{0:T(1024)}, u32[]{:S(2)}) copy-start(f32[1024]{0:T(1024)} %param.11) | copy-start | bytes 12292
  212.5 258.6 %reduce-scatter.4.cloned.1.call-start = ((), (), s32[]{:S(2)}) async-start(), calls=%async_computation.4 | async-start | bytes 208896
  472.6 7.0 %all-to-all-start.1 = ((f32[2,1,192]{2,1,0:T(1,128)}), f32[2,1,192]{2,1,0:T(1,128)S(1)}, u32[]{:S(2)}, u32[]{:S(2)}) async-start(f32[2,1,192]{2,1,0:T(1,128)} %reshape.46), calls=%async_computation.1 | async-start | bytes 4096 | tf_op jit(solution)/shard_map/all_to_all | solution.py:35
Sparse Core Ops, SparseCore 0:
  212.7 153.5 all-gather.1
  417.5 53.5 reduce-scatter.3
where the time goes:
time: 490 us; the launch traced here: 489 us
  waiting for transfers between devices  210 us (43%)
  blocking collectives  189 us (39%)
  matrix products  50.3 us (10%)
  local copies, waits for them, and re-layouts  19.7 us (4%)
  between operations  13.5 us (3%)
    all_to_all x1, blocking collectives, shards(): lax.all_to_all(amplitudes, 'wide', split_axis=1, concat_axis=0, tiled=True)  189 us
    all_gather x1, waiting for transfers between devices, shards(): lax.all_gather(exchanged, 'narrow', axis=2, tiled=True)  153 us
    unnamed x3, waiting for transfers between devices  53.7 us
    dot_general x1, matrix products, contract(): lax.dot_general(left_rows.reshape(left_rows.shape[0], -1), right_rows.res...  50.3 us
  transfers between devices with their start and end apart: 3, of which 3 were waited for; matrix products, arithmetic and copies ran while one was open for 0% of the time, Pallas kernels for 0%

commit v1 on v0

--- a/solution.py
+++ b/solution.py
@@ -2,6 +2,30 @@
 import jax.numpy as jnp
 from jax import lax
 from jax.sharding import PartitionSpec as P
+
+
+def in_blocks(array, dim, size):
+    shape = array.shape
+    tiles = array.reshape(*shape[:dim], size, shape[dim] // size, *shape[dim + 1 :])
+    return jnp.moveaxis(tiles, dim, 0)
+
+
+def laid_out(pieces, dim):
+    dims = list(pieces.shape[1:])
+    dims[dim] *= pieces.shape[0]
+    return jnp.moveaxis(pieces, 0, dim).reshape(dims)
+
+
+def rotated_exchange(x, axis, split_dim, concat_dim):
+    peers, index = (lax.axis_size(axis), lax.axis_index(axis))
+    blocks = in_blocks(x, split_dim, peers)
+    result = blocks
+    for step in range(1, peers):
+        target, source = ((index + step) % peers, (index - step) % peers)
+        sent = lax.dynamic_index_in_dim(blocks, target, 0)
+        other = lax.ppermute(sent, axis, [(i, (i + step) % peers) for i in range(peers)])
+        result = lax.dynamic_update_slice_in_dim(result, other, source, axis=0)
+    return laid_out(result, concat_dim)
 
 
 def lookup(table, indices):
@@ -22,7 +46,7 @@
 
 
 def shards(amplitudes, integrals, pair_index, window_virtuals, occ_energy, virt_energy):
-    exchanged = lax.all_to_all(amplitudes, "wide", split_axis=1, concat_axis=0, tiled=True)
+    exchanged = rotated_exchange(amplitudes, "wide", 1, 0)
     rows_here = integrals.shape[0]
     window = integrals.shape[1]
     first_block = integrals.shape[2]

time: 490 us -> 457 us (0.933)
  blocking collectives: 189 us -> 0 us
  starting transfers between devices: 3.26 us -> 72.8 us
  local copies, waits for them, and re-layouts: 19.7 us -> 86.9 us
  waiting for transfers between devices: 210 us -> 242 us
  matrix products: 50.3 us -> 39.2 us
    all_to_all x1 -> x0, blocking collectives: 189 us -> none  [shards(): lax.all_to_all(amplitudes, 'wide', split_axis=1, concat_axis=0, tiled=True)]
    ppermute x0 -> x15, starting transfers between devices: none -> 69.4 us  [rotated_exchange(): lax.ppermute(sent, axis, [(i, (i + step) % peers) for i in range(peers)])]
    ppermute x0 -> x15, waiting for transfers between devices: none -> 63.2 us  [rotated_exchange(): lax.ppermute(sent, axis, [(i, (i + step) % peers) for i in range(peers)])]
    unnamed x11 -> x13, local copies, waits for them, and re-layouts: 7.9 us -> 56.5 us
    all_gather x1, waiting for transfers between devices: 153 us -> 121 us  [shards(): lax.all_gather(exchanged, 'narrow', axis=2, tiled=True)]
    dynamic_update_slice x0 -> x16, local copies, waits for them, and re-layouts: none -> 23.3 us  [rotated_exchange(): result = lax.dynamic_update_slice_in_dim(result, other, source, axis=0)]
    dot_general x1, matrix products: 50.3 us -> 39.2 us  [contract(): lax.dot_general(left_rows.reshape(left_rows.shape[0], -1), right_rows.res...]
    all_to_all x3 -> x0, local copies, waits for them, and re-layouts: 9.52 us -> none  [shards(): lax.all_to_all(amplitudes, 'wide', split_axis=1, concat_axis=0, tiled=True)]
  transfers between devices with their start and end apart: 3 -> 18, of which waited for: 3 -> 7; matrix products, arithmetic and copies ran while one was open for 0% -> 11% of each run, Pallas kernels for 0% -> 0%
where the time goes in v1:
time: 457 us
  waiting for transfers between devices  242 us (53%)
  local copies, waits for them, and re-layouts  86.9 us (19%)
  starting transfers between devices  72.8 us (16%)
  matrix products  39.2 us (9%)
  between operations  13.5 us (3%)
    all_gather x1, waiting for transfers between devices, shards(): lax.all_gather(exchanged, 'narrow', axis=2, tiled=True)  121 us
    ppermute x15, starting transfers between devices, rotated_exchange(): lax.ppermute(sent, axis, [(i, (i + step) % peers) for i in range(peers)])  69.4 us
    ppermute x15, waiting for transfers between devices, rotated_exchange(): lax.ppermute(sent, axis, [(i, (i + step) % peers) for i in range(peers)])  63.2 us
    unnamed x13, local copies, waits for them, and re-layouts  56.5 us
    unnamed x3, waiting for transfers between devices  53.7 us
    dot_general x1, matrix products, contract(): lax.dot_general(left_rows.reshape(left_rows.shape[0], -1), right_rows.res...  39.2 us
    dynamic_update_slice x16, local copies, waits for them, and re-layouts, rotated_exchange(): result = lax.dynamic_update_slice_in_dim(result, other, source, axis=0)  23.3 us
  transfers between devices with their start and end apart: 18, of which 7 were waited for; matrix products, arithmetic and copies ran while one was open for 11% of the time, Pallas kernels for 0%

profile of v1, /device:TPU:0, one launch (start us, length us, event | category | flops | bytes accessed | tf_op | source)
XLA Modules:
  0.0 456.7 jit_solution(13121294733640293098)
XLA Ops:
  6.5 6.1 %copy.45 = f32[3,1024,512]{2,1,0:T(8,128)} copy(f32[3,1024,512]{2,1,0:T(8,128)} %param.6) | data formatting | bytes 12582912
  12.7 4.7 %dynamic-slice_bitcast_fusion = (f32[1,3,64,512]{3,2,0,1:T(8,128)S(1)}, f32[1,3,64,512]{3,2,0,1:T(8,128)S(1)}, f32[1,3,64,512]{3,2,0,1:T(8,128)S(1)}, f32[1,3,64...) fusion(f32[3,16,64,512]{3,2,1,0:T(8,128)} %bitcast.63, ...), kind=kLoop, calls=%fused_computation.1 | loop fusion | bytes 11796540 | tf_op jit(solution)/shard_map/jit(dynamic_index_in_dim)/dynamic_slice | solution.py:25
  17.8 2.5 collective-permute-start.1
  20.4 2.4 collective-permute-start.2
  22.8 1.6 collective-permute-start.3
  24.5 7.4 %collective-permute-done = f32[1,3,64,512]{3,2,0,1:T(8,128)} collective-permute-done((f32[1,3,64,512]{3,2,0,1:T(8,128)}, f32[1,3,64,512]{3,2,0,1:T(8,128)}, u32[]{:S(2)}, u32[]{:S(2)}) %collective-permute-start) | collective-permute-done | bytes 393248 | tf_op jit(solution)/shard_map/ppermute | solution.py:26
  32.5 1.8 constant_dynamic-update-slice_fusion.14
  34.2 7.3 %collective-permute-start.6 = (f32[1,3,64,512]{3,2,0,1:T(8,128)S(1)}, f32[1,3,64,512]{3,2,0,1:T(8,128)S(1)}, u32[]{:S(2)}, u32[]{:S(2)}) collective-permute-start(f32[1,3,64,512]{3,2,0,1:T(8,128)S(1)} %get-tuple-element.15), channel_id=1, source_target_pairs={{0,14},{2,16},{4,18},{6,20},{8,22},{10,24},{12,26},{14,28},{16,30}... | collective-permute-start | bytes 1179656 | tf_op jit(solution)/shard_map/ppermute | solution.py:26
  41.6 1.8 constant_dynamic-update-slice_fusion.13
  43.3 1.7 collective-permute-start.7
  45.0 1.8 constant_dynamic-update-slice_fusion.12
  46.8 1.8 constant_dynamic-update-slice_fusion.11
  48.6 51.5 %collective-permute-done.4 = f32[1,3,64,512]{3,2,0,1:T(8,128)} collective-permute-done((f32[1,3,64,512]{3,2,0,1:T(8,128)}, f32[1,3,64,512]{3,2,0,1:T(8,128)}, u32[]{:S(2)}, u32[]{:S(2)}) %collective-permute-start.4) | collective-permute-done | bytes 393248 | tf_op jit(solution)/shard_map/ppermute | solution.py:26
  100.1 1.8 constant_dynamic-update-slice_fusion.10
  101.9 10.0 %collective-permute-start.10 = (f32[1,3,64,512]{3,2,0,1:T(8,128)S(1)}, f32[1,3,64,512]{3,2,0,1:T(8,128)S(1)}, u32[]{:S(2)}, u32[]{:S(2)}) collective-permute-start(f32[1,3,64,512]{3,2,0,1:T(8,128)S(1)} %get-tuple-element.11), channel_id=1, source_target_pairs={{0,22},{2,24},{4,26},{6,28},{8,30},{10,0},{12,2},{14,4},{16,6},{18... | collective-permute-start | bytes 1179656 | tf_op jit(solution)/shard_map/ppermute | solution.py:26
  112.6 18.7 %collective-permute-start.11 = (f32[1,3,64,512]{3,2,0,1:T(8,128)S(1)}, f32[1,3,64,512]{3,2,0,1:T(8,128)S(1)}, u32[]{:S(2)}, u32[]{:S(2)}) collective-permute-start(f32[1,3,64,512]{3,2,0,1:T(8,128)S(1)} %get-tuple-element.10), channel_id=1, source_target_pairs={{0,24},{2,26},{4,28},{6,30},{8,0},{10,2},{12,4},{14,6},{16,8},{18,... | collective-permute-start | bytes 1179656 | tf_op jit(solution)/shard_map/ppermute | solution.py:26
  131.3 0.8 constant_dynamic-update-slice_fusion.8
  133.3 12.4 %collective-permute-start.13 = (f32[1,3,64,512]{3,2,0,1:T(8,128)S(1)}, f32[1,3,64,512]{3,2,0,1:T(8,128)S(1)}, u32[]{:S(2)}, u32[]{:S(2)}) collective-permute-start(f32[1,3,64,512]{3,2,0,1:T(8,128)S(1)} %get-tuple-element.8), channel_id=1, source_target_pairs={{0,28},{2,30},{4,0},{6,2},{8,4},{10,6},{12,8},{14,10},{16,12},{18,... | collective-permute-start | bytes 1179656 | tf_op jit(solution)/shard_map/ppermute | solution.py:26
  146.5 11.2 %collective-permute-start.14 = (f32[1,3,64,512]{3,2,0,1:T(8,128)S(1)}, f32[1,3,64,512]{3,2,0,1:T(8,128)S(1)}, u32[]{:S(2)}, u32[]{:S(2)}) collective-permute-start(f32[1,3,64,512]{3,2,0,1:T(8,128)S(1)} %get-tuple-element.7), channel_id=1, source_target_pairs={{0,30},{2,0},{4,2},{6,4},{8,6},{10,8},{12,10},{14,12},{16,14},{18,... | collective-permute-start | bytes 1179656 | tf_op jit(solution)/shard_map/ppermute | solution.py:26
  157.7 0.8 constant_dynamic-update-slice_fusion.5
  160.9 2.4 collective-permute-done.13
  164.0 1.8 collective-permute-done.14
  166.6 6.6 %copy.20 = f32[16,3,64,512]{3,2,1,0:T(8,128)} copy(f32[16,3,64,512]{3,2,0,1:T(8,128)} %constant_dynamic-update-slice_fusion) | data formatting | bytes 12582912 | tf_op jit(solution)/shard_map/dynamic_update_slice | solution.py:27
  173.6 33.1 %copy.26 = f32[16,8,64,1024]{3,1,2,0:T(8,128)} copy(f32[16,8,64,1024]{3,2,1,0:T(8,128)} %bitcast.65) | data formatting | bytes 67108864
  207.2 121.1 %all-gather.2.cloned.1.call-done = f32[48,64,1024]{2,1,0:T(8,128)} async-done(((f32[48,64,512]{2,1,0:T(8,128)}), f32[48,64,1024]{2,1,0:T(8,128)}) %all-gather.2.cloned.1.call-update) | async-done | bytes 12582928 | tf_op jit(solution)/shard_map/all_gather | solution.py:55
  328.3 16.5 %copy.25 = f32[6,8,64,1024]{3,1,2,0:T(8,128)} copy(f32[6,8,64,1024]{3,2,1,0:T(8,128)} %bitcast.67) | data formatting | bytes 25165824
  344.8 39.2 %convolution_bitcast_fusion = f32[128,48]{0,1:T(8,128)S(1)} fusion(f32[48,65536]{1,0:T(8,128)} %bitcast.62, f32[128,65536]{1,0:T(8,128)} %bitcast.61), kind=kOutput, calls=%fused_computation | convolution fusion | flops 4831838208 | bytes 46161920 | tf_op jit(solution)/shard_map/dot_general | solution.py:39
  384.0 0.8 copy.22
  384.9 53.7 %reduce-scatter.4.cloned.1.call-done = f32[8,16,3]{1,0,2:T(8,128)} async-done(((f32[8,16,48]{1,0,2:T(8,128)}), f32[8,16,3]{1,0,2:T(8,128)}) %reduce-scatter.4.cloned.1.call-update) | async-done | bytes 1552
  440.1 3.2 all-to-all-start
  443.5 3.6 all-to-all-done
  448.4 1.4 fusion
  (52 shorter events, 11.7 us)
Async XLA Ops:
  6.5 321.8 %all-gather.2.cloned.1.call-start = ((), (), s32[]{:S(2)}) async-start(), calls=%async_computation.2 | async-start | bytes 18874368 | tf_op jit(solution)/shard_map/all_gather | solution.py:55
  17.4 14.6 %collective-permute-start = (f32[1,3,64,512]{3,2,0,1:T(8,128)}, f32[1,3,64,512]{3,2,0,1:T(8,128)}, u32[]{:S(2)}, u32[]{:S(2)}) collective-permute-start(f32[1,3,64,512]{3,2,0,1:T(8,128)} %get-tuple-element.21), channel_id=1, source_target_pairs={{0,2},{2,4},{4,6},{6,8},{8,10},{10,12},{12,14},{14,16},{16,18},{18... | collective-permute-start | bytes 1179656 | tf_op jit(solution)/shard_map/ppermute | solution.py:26
  17.8 16.4 %collective-permute-start.1 = (f32[1,3,64,512]{3,2,0,1:T(8,128)}, f32[1,3,64,512]{3,2,0,1:T(8,128)}, u32[]{:S(2)}, u32[]{:S(2)}) collective-permute-start(f32[1,3,64,512]{3,2,0,1:T(8,128)} %get-tuple-element.20), channel_id=1, source_target_pairs={{0,4},{2,6},{4,8},{6,10},{8,12},{10,14},{12,16},{14,18},{16,20},{1... | collective-permute-start | bytes 1179656 | tf_op jit(solution)/shard_map/ppermute | solution.py:26
  20.4 23.0 %collective-permute-start.2 = (f32[1,3,64,512]{3,2,0,1:T(8,128)}, f32[1,3,64,512]{3,2,0,1:T(8,128)}, u32[]{:S(2)}, u32[]{:S(2)}) collective-permute-start(f32[1,3,64,512]{3,2,0,1:T(8,128)} %get-tuple-element.19), channel_id=1, source_target_pairs={{0,6},{2,8},{4,10},{6,12},{8,14},{10,16},{12,18},{14,20},{16,22},{... | collective-permute-start | bytes 1179656 | tf_op jit(solution)/shard_map/ppermute | solution.py:26
  22.8 24.0 %collective-permute-start.3 = (f32[1,3,64,512]{3,2,0,1:T(8,128)}, f32[1,3,64,512]{3,2,0,1:T(8,128)}, u32[]{:S(2)}, u32[]{:S(2)}) collective-permute-start(f32[1,3,64,512]{3,2,0,1:T(8,128)} %get-tuple-element.18), channel_id=1, source_target_pairs={{0,8},{2,10},{4,12},{6,14},{8,16},{10,18},{12,20},{14,22},{16,24},... | collective-permute-start | bytes 1179656 | tf_op jit(solution)/shard_map/ppermute | solution.py:26
  24.4 75.7 %collective-permute-start.4 = (f32[1,3,64,512]{3,2,0,1:T(8,128)}, f32[1,3,64,512]{3,2,0,1:T(8,128)}, u32[]{:S(2)}, u32[]{:S(2)}) collective-permute-start(f32[1,3,64,512]{3,2,0,1:T(8,128)} %get-tuple-element.17), channel_id=1, source_target_pairs={{0,10},{2,12},{4,14},{6,16},{8,18},{10,20},{12,22},{14,24},{16,26}... | collective-permute-start | bytes 1179656 | tf_op jit(solution)/shard_map/ppermute | solution.py:26
  32.0 69.9 %collective-permute-start.5 = (f32[1,3,64,512]{3,2,0,1:T(8,128)}, f32[1,3,64,512]{3,2,0,1:T(8,128)S(1)}, u32[]{:S(2)}, u32[]{:S(2)}) collective-permute-start(f32[1,3,64,512]{3,2,0,1:T(8,128)} %get-tuple-element.16), channel_id=1, source_target_pairs={{0,12},{2,14},{4,16},{6,18},{8,20},{10,22},{12,24},{14,26},{16,28}... | collective-permute-start | bytes 1179656 | tf_op jit(solution)/shard_map/ppermute | solution.py:26
  34.2 78.4 %collective-permute-start.6 = (f32[1,3,64,512]{3,2,0,1:T(8,128)S(1)}, f32[1,3,64,512]{3,2,0,1:T(8,128)S(1)}, u32[]{:S(2)}, u32[]{:S(2)}) collective-permute-start(f32[1,3,64,512]{3,2,0,1:T(8,128)S(1)} %get-tuple-element.15), channel_id=1, source_target_pairs={{0,14},{2,16},{4,18},{6,20},{8,22},{10,24},{12,26},{14,28},{16,30}... | collective-permute-start | bytes 1179656 | tf_op jit(solution)/shard_map/ppermute | solution.py:26
  43.3 88.8 %collective-permute-start.7 = (f32[1,3,64,512]{3,2,0,1:T(8,128)S(1)}, f32[1,3,64,512]{3,2,0,1:T(8,128)S(1)}, u32[]{:S(2)}, u32[]{:S(2)}) collective-permute-start(f32[1,3,64,512]{3,2,0,1:T(8,128)S(1)} %get-tuple-element.14), channel_id=1, source_target_pairs={{0,16},{2,18},{4,20},{6,22},{8,24},{10,26},{12,28},{14,30},{16,0},... | collective-permute-start | bytes 1179656 | tf_op jit(solution)/shard_map/ppermute | solution.py:26
  46.8 86.6 %collective-permute-start.8 = (f32[1,3,64,512]{3,2,0,1:T(8,128)S(1)}, f32[1,3,64,512]{3,2,0,1:T(8,128)S(1)}, u32[]{:S(2)}, u32[]{:S(2)}) collective-permute-start(f32[1,3,64,512]{3,2,0,1:T(8,128)S(1)} %get-tuple-element.13), channel_id=1, source_target_pairs={{0,18},{2,20},{4,22},{6,24},{8,26},{10,28},{12,30},{14,0},{16,2},{... | collective-permute-start | bytes 1179656 | tf_op jit(solution)/shard_map/ppermute | solution.py:26
  100.1 46.4 %collective-permute-start.9 = (f32[1,3,64,512]{3,2,0,1:T(8,128)S(1)}, f32[1,3,64,512]{3,2,0,1:T(8,128)S(1)}, u32[]{:S(2)}, u32[]{:S(2)}) collective-permute-start(f32[1,3,64,512]{3,2,0,1:T(8,128)S(1)} %get-tuple-element.12), channel_id=1, source_target_pairs={{0,20},{2,22},{4,24},{6,26},{8,28},{10,30},{12,0},{14,2},{16,4},{1... | collective-permute-start | bytes 1179656 | tf_op jit(solution)/shard_map/ppermute | solution.py:26
  101.9 56.7 %collective-permute-start.10 = (f32[1,3,64,512]{3,2,0,1:T(8,128)S(1)}, f32[1,3,64,512]{3,2,0,1:T(8,128)S(1)}, u32[]{:S(2)}, u32[]{:S(2)}) collective-permute-start(f32[1,3,64,512]{3,2,0,1:T(8,128)S(1)} %get-tuple-element.11), channel_id=1, source_target_pairs={{0,22},{2,24},{4,26},{6,28},{8,30},{10,0},{12,2},{14,4},{16,6},{18... | collective-permute-start | bytes 1179656 | tf_op jit(solution)/shard_map/ppermute | solution.py:26
  112.6 46.7 %collective-permute-start.11 = (f32[1,3,64,512]{3,2,0,1:T(8,128)S(1)}, f32[1,3,64,512]{3,2,0,1:T(8,128)S(1)}, u32[]{:S(2)}, u32[]{:S(2)}) collective-permute-start(f32[1,3,64,512]{3,2,0,1:T(8,128)S(1)} %get-tuple-element.10), channel_id=1, source_target_pairs={{0,24},{2,26},{4,28},{6,30},{8,0},{10,2},{12,4},{14,6},{16,8},{18,... | collective-permute-start | bytes 1179656 | tf_op jit(solution)/shard_map/ppermute | solution.py:26
  132.1 28.0 %collective-permute-start.12 = (f32[1,3,64,512]{3,2,0,1:T(8,128)S(1)}, f32[1,3,64,512]{3,2,0,1:T(8,128)S(1)}, u32[]{:S(2)}, u32[]{:S(2)}) collective-permute-start(f32[1,3,64,512]{3,2,0,1:T(8,128)S(1)} %get-tuple-element.9), channel_id=1, source_target_pairs={{0,26},{2,28},{4,30},{6,0},{8,2},{10,4},{12,6},{14,8},{16,10},{18,... | collective-permute-start | bytes 1179656 | tf_op jit(solution)/shard_map/ppermute | solution.py:26
  133.3 29.9 %collective-permute-start.13 = (f32[1,3,64,512]{3,2,0,1:T(8,128)S(1)}, f32[1,3,64,512]{3,2,0,1:T(8,128)S(1)}, u32[]{:S(2)}, u32[]{:S(2)}) collective-permute-start(f32[1,3,64,512]{3,2,0,1:T(8,128)S(1)} %get-tuple-element.8), channel_id=1, source_target_pairs={{0,28},{2,30},{4,0},{6,2},{8,4},{10,6},{12,8},{14,10},{16,12},{18,... | collective-permute-start | bytes 1179656 | tf_op jit(solution)/shard_map/ppermute | solution.py:26
  146.5 19.3 %collective-permute-start.14 = (f32[1,3,64,512]{3,2,0,1:T(8,128)S(1)}, f32[1,3,64,512]{3,2,0,1:T(8,128)S(1)}, u32[]{:S(2)}, u32[]{:S(2)}) collective-permute-start(f32[1,3,64,512]{3,2,0,1:T(8,128)S(1)} %get-tuple-element.7), channel_id=1, source_target_pairs={{0,30},{2,0},{4,2},{6,4},{8,6},{10,8},{12,10},{14,12},{16,14},{18,... | collective-permute-start | bytes 1179656 | tf_op jit(solution)/shard_map/ppermute | solution.py:26
  173.3 265.3 %reduce-scatter.4.cloned.1.call-start = ((), (), s32[]{:S(2)}) async-start(), calls=%async_computation.3 | async-start | bytes 208896
  173.5 33.2 %copy-start.3 = (s32[16]{0:T(128)S(1)}, s32[16]{0:T(128)}, u32[]{:S(2)}) copy-start(s32[16]{0:T(128)} %param.9) | copy-start | bytes 196
  173.5 33.3 %copy-start.2 = (s32[3,2]{0,1:T(2,128)S(1)}, s32[3,2]{0,1:T(2,128)}, u32[]{:S(2)}) copy-start(s32[3,2]{0,1:T(2,128)} %param.8) | copy-start | bytes 76
  173.5 33.3 %copy-start.1 = (f32[200]{0:T(256)S(1)}, f32[200]{0:T(256)}, u32[]{:S(2)}) copy-start(f32[200]{0:T(256)} %param.10) | copy-start | bytes 2404
  173.5 33.5 %copy-start = (f32[1024]{0:T(1024)S(1)}, f32[1024]{0:T(1024)}, u32[]{:S(2)}) copy-start(f32[1024]{0:T(1024)} %param.11) | copy-start | bytes 12292
  440.1 7.0 %all-to-all-start = ((f32[2,1,192]{2,1,0:T(1,128)}), f32[2,1,192]{2,1,0:T(1,128)S(1)}, u32[]{:S(2)}, u32[]{:S(2)}) async-start(f32[2,1,192]{2,1,0:T(1,128)} %reshape.71), calls=%async_computation | async-start | bytes 4096 | tf_op jit(solution)/shard_map/all_to_all | solution.py:59
Sparse Core Ops, SparseCore 0:
  173.4 154.8 all-gather.1
  385.0 53.5 reduce-scatter.3
